TPU v7x, 32 devices: a whole 2x2x4 slice. The times are simulated.
32 devices in a mesh: energy: 4 (over x, core), slab: 8 (over z, y).
Axes of the slice: x: 2, y: 2, z: 4, core: 2. Of those that a mesh axis runs over, the one named last changes fastest.
Arguments:
- g_lesser: bfloat16 [4, 8, 3, 2, 256, 256], P('energy', 'slab'), may hold values from -6 to 6
- g_greater: bfloat16 [4, 8, 3, 2, 256, 256], P('energy', 'slab'), may hold values from -6 to 6
- v_diag: bfloat16 [8, 2, 256, 256], P('slab'), may hold values from -0.15625 to 0.15625
- v_upper: bfloat16 [8, 2, 256, 256], P('slab'), may hold values from -0.15625 to 0.15625
Outputs:
- w_diag: bfloat16 [4, 8, 2, 256, 256], P('energy', 'slab')
- w_upper: bfloat16 [4, 8, 2, 256, 256], P('energy', 'slab')
All inputs are finite; a program needn't handle non-finite values.
Results may differ from a plain program's by a relative error of at most 0.0058.
Values may be sent and summed in bfloat16 or wider, within the bound.
No kernel may reach another device: no remote copies, remote signals or barrier semaphores. Data moves between devices by JAX's collectives and lax.ppermute only.
A program may use at most 64 MiB of HBM per device.

v0:
```python
import math
import jax
import jax.numpy as jnp
from jax import lax
from jax.sharding import PartitionSpec as P


def extended(shard, sides, width):
    for axis, dim in sides:
        count, length = (lax.axis_size(axis), shard.shape[dim])
        up = [(i, (i + 1) % count) for i in range(count - 1)]
        down = [(j, i) for i, j in up]
        last = lax.slice_in_dim(shard, length - width, length, axis=dim)
        initial = lax.slice_in_dim(shard, 0, width, axis=dim)
        before = lax.ppermute(last, axis, up)
        after = lax.ppermute(initial, axis, down)
        shard = jnp.concatenate([before, shard, after], axis=dim)
    return shard


def passed_along(value, axis, steps):
    count = lax.axis_size(axis)
    initial, last = (max(0, -steps), min(count, count - steps))
    return lax.ppermute(value, axis, [(source, source + steps) for source in range(initial, last)])


def complex_product(left_block, right_block, left_adjoint=False, right_adjoint=False):
    left_re = left_block[..., 0, :, :]
    left_im = left_block[..., 1, :, :]
    right_re = right_block[..., 0, :, :]
    right_im = right_block[..., 1, :, :]
    pattern = (
        ("...ji" if left_adjoint else "...ij")
        + ","
        + ("...kj" if right_adjoint else "...jk")
        + "->...ik"
    )

    def contract(first_part, second_part):
        return jnp.einsum(pattern, first_part, second_part, preferred_element_type=jnp.float32)

    left_sign = -1.0 if left_adjoint else 1.0
    right_sign = -1.0 if right_adjoint else 1.0
    real_part = contract(left_re, right_re) - left_sign * right_sign * contract(left_im, right_im)
    imag_part = right_sign * contract(left_re, right_im) + left_sign * contract(left_im, right_re)
    return jnp.stack([real_part, imag_part], axis=-3)


def transform(table, signal):
    return jnp.einsum("fn,n...->f...", table, signal, precision=lax.Precision.HIGH)


def correlate(pieces):
    lesser, greater = pieces
    energies = lesser.shape[0]
    length = 2 * energies
    frequency = jnp.arange(length, dtype=jnp.int32)
    energy_ids = jnp.arange(energies, dtype=jnp.int32)
    step_angle = 2.0 * math.pi / length
    forward_angle = (frequency[:, None] * energy_ids[None, :] % length).astype(
        jnp.float32
    ) * step_angle
    shifts = energy_ids - energies // 2
    inverse_angle = (shifts[:, None] * frequency[None, :] % length).astype(jnp.float32) * step_angle
    forward_cos = jnp.cos(forward_angle)
    forward_sin = jnp.sin(forward_angle)
    inverse_cos = jnp.cos(inverse_angle)
    inverse_sin = jnp.sin(inverse_angle)

    def spectrum(signal):
        signal_re = signal[:, :, :, 0].astype(jnp.float32)
        signal_im = signal[:, :, :, 1].astype(jnp.float32)
        spec_re = transform(forward_cos, signal_re) + transform(forward_sin, signal_im)
        spec_im = transform(forward_cos, signal_im) - transform(forward_sin, signal_re)
        return (spec_re, spec_im)

    lesser_re, lesser_im = spectrum(lesser)
    greater_re, greater_im = spectrum(greater)
    cross_re = lesser_re * greater_re + lesser_im * greater_im
    cross_im = lesser_im * greater_re - lesser_re * greater_im
    corr_re = (transform(inverse_cos, cross_re) - transform(inverse_sin, cross_im)) / length
    corr_im = (transform(inverse_cos, cross_im) + transform(inverse_sin, cross_re)) / length
    factor = 1.0 / math.sqrt(energies)
    polar_entries = jnp.stack([-corr_im * factor, corr_re * factor], axis=3).astype(jnp.bfloat16)
    return lax.all_to_all(polar_entries, "energy", split_axis=0, concat_axis=4, tiled=True)


def per_device(g_lesser, g_greater, v_diag, v_upper):
    local_rows = v_diag.shape[0]
    total_rows = local_rows * lax.axis_size("slab")
    first_row = lax.axis_index("slab") * local_rows
    inside = first_row + jnp.arange(local_rows, dtype=jnp.int32) < total_rows - 1
    inside = inside.astype(jnp.bfloat16)[:, None, None, None]
    coupling = jnp.stack([v_diag, v_upper * inside], axis=1)
    padded = extended(coupling, (("slab", 0),), 1)
    diag_below = padded[:-2, 0][None]
    diag_middle = padded[1:-1, 0][None]
    diag_above = padded[2:, 0][None]
    upper_below = padded[:-2, 1][None]
    upper_middle = padded[1:-1, 1][None]
    upper_above = padded[2:, 1][None]
    middle = correlate(
        (
            lax.all_to_all(g_lesser, "energy", split_axis=4, concat_axis=0, tiled=True),
            lax.all_to_all(g_greater, "energy", split_axis=4, concat_axis=0, tiled=True),
        )
    )
    toward_above_y = complex_product(middle[:, :, 1], upper_middle) + complex_product(
        middle[:, :, 2], diag_above
    )
    toward_above_z = complex_product(middle[:, :, 2], upper_above)
    toward_below_y = complex_product(middle[:, :, 0], diag_below) + complex_product(
        middle[:, :, 1], upper_below, False, True
    )
    toward_below_z = (
        complex_product(middle[:, :, 0], upper_below)
        + complex_product(middle[:, :, 1], diag_middle)
        + complex_product(middle[:, :, 2], upper_middle, False, True)
    )
    sent_up = jnp.stack([toward_above_y, toward_above_z], axis=2).astype(jnp.bfloat16)
    sent_down = jnp.stack([toward_below_y, toward_below_z], axis=2).astype(jnp.bfloat16)
    arrived_below = passed_along(sent_up[:, -1:], "slab", 1)
    from_below = jnp.concatenate([arrived_below, sent_up[:, :-1]], axis=1)
    arrived_above = passed_along(sent_down[:, :1], "slab", -1)
    from_above = jnp.concatenate([sent_down[:, 1:], arrived_above], axis=1)
    below_y = from_below[:, :, 0]
    below_z = from_below[:, :, 1]
    above_y = from_above[:, :, 0]
    above_z = from_above[:, :, 1]
    middle_y = (
        complex_product(middle[:, :, 0], upper_below)
        + complex_product(middle[:, :, 1], diag_middle)
        + complex_product(middle[:, :, 2], upper_middle, False, True)
    ).astype(jnp.bfloat16)
    middle_z = (
        complex_product(middle[:, :, 1], upper_middle)
        + complex_product(middle[:, :, 2], diag_above)
    ).astype(jnp.bfloat16)
    w_diag = (
        complex_product(upper_below, below_y, True, False)
        + complex_product(diag_middle, middle_y)
        + complex_product(upper_middle, above_y)
    ).astype(jnp.bfloat16)
    w_upper = (
        complex_product(upper_below, below_z, True, False)
        + complex_product(diag_middle, middle_z)
        + complex_product(upper_middle, above_z)
    ).astype(jnp.bfloat16)
    return (w_diag, w_upper)


def solution(mesh):
    placed = (
        P("energy", "slab", None, None, None, None),
        P("energy", "slab", None, None, None, None),
        P("slab", None, None, None),
        P("slab", None, None, None),
    )
    return jax.shard_map(
        per_device,
        mesh=mesh,
        in_specs=placed,
        out_specs=(P("energy", "slab", None, None, None), P("energy", "slab", None, None, None)),
        check_vma=False,
    )
```

profile of v0, /device:TPU:26, one launch (start us, length us, event | category | flops | bytes accessed | tf_op | source)
XLA Modules:
  0.0 119.2 jit_solution(980924947038684042)
XLA Ops:
  0.6 2.9 %copy.44 = bf16[1,1,3,2,256,256]{5,2,3,1,0,4:T(4,128)(2,1)} copy(bf16[1,1,3,2,256,256]{5,4,3,2,1,0:T(8,128)(2,1)} %param.5) | data formatting | bytes 1572864 | tf_op args[1]
  3.5 4.0 %all-to-all-start.1 = ((bf16[1,1,3,2,256,256]{5,2,3,1,0,4:T(4,128)(2,1)}), bf16[1,1,3,2,256,256]{5,2,3,1,0,4:T(4,128)(2,1)S(1)}, u32[]{:S(2)}, u32[]{:S(2)}) async-start(bf16[1,1,3,2,256,256]{5,2,3,1,0,4:T(4,128)(2,1)} %copy.44), calls=%async_computation.1 | async-start | bytes 2097152 | tf_op jit(solution)/shard_map/all_to_all | solution.py:105
  7.5 1.7 %copy.41 = bf16[1,1,3,2,256,256]{5,2,3,1,0,4:T(4,128)(2,1)} copy(bf16[1,1,3,2,256,256]{5,4,3,2,1,0:T(8,128)(2,1)S(1)} %copy-done.2) | data formatting | bytes 1572864 | tf_op args[0]
  9.2 11.1 %all-to-all-done.1 = bf16[1,1,3,2,256,256]{5,2,3,1,0,4:T(4,128)(2,1)S(1)} async-done(((bf16[1,1,3,2,256,256]{5,2,3,1,0,4:T(4,128)(2,1)}), bf16[1,1,3,2,256,256]{5,2,3,1,0,4:T(4,128)(2,1)S(1)}, u32[]{:S(2)}, u32[]{:S(2)}) %all-to-all-start.1) | async-done | bytes 786464 | tf_op jit(solution)/shard_map/all_to_all | solution.py:105
  20.3 5.1 %all-to-all-start = ((bf16[1,1,3,2,256,256]{5,2,3,1,0,4:T(4,128)(2,1)}), bf16[1,1,3,2,256,256]{5,2,3,1,0,4:T(4,128)(2,1)S(1)}, u32[]{:S(2)}, u32[]{:S(2)}) async-start(bf16[1,1,3,2,256,256]{5,2,3,1,0,4:T(4,128)(2,1)} %copy.41), calls=%async_computation | async-start | bytes 2097152 | tf_op jit(solution)/shard_map/all_to_all | solution.py:104
  26.2 1.9 %fusion.43 = f32[8,3,64,256]{3,0,2,1:T(8,128)} fusion(bf16[4,1,3,2,64,256]{5,0,4,2,3,1:T(4,128)(2,1)S(1)} %bitcast.359), kind=kOutput, calls=%fused_computation.102 | convolution fusion | flops 9437632 | bytes 1966080 | tf_op jit(solution)/shard_map/fn,n...->f.../dot_general | solution.py:50
  28.8 9.4 %all-to-all-done = bf16[1,1,3,2,256,256]{5,2,3,1,0,4:T(4,128)(2,1)S(1)} async-done(((bf16[1,1,3,2,256,256]{5,2,3,1,0,4:T(4,128)(2,1)}), bf16[1,1,3,2,256,256]{5,2,3,1,0,4:T(4,128)(2,1)S(1)}, u32[]{:S(2)}, u32[]{:S(2)}) %all-to-all-start) | async-done | bytes 786464 | tf_op jit(solution)/shard_map/all_to_all | solution.py:104
  42.1 0.8 convolution_subtract_fusion
  42.9 1.2 %multiply_subtract_fusion = (f32[8,3,64,256]{3,0,2,1:T(8,128)S(1)}, f32[8,3,64,256]{3,0,2,1:T(8,128)S(1)}) fusion(f32[8,3,64,256]{3,0,2,1:T(8,128)S(1)} %convolution_subtract_fusion, f32[8,3,64,256]{3,0,2,1:T(8,128)S(1)} %convolution_subtract_fusion.1, f32[8,3,64,256]{3,0,2,1:T(8,128)S(1)} %convolution_add_fusion.1, f32[8,3,64,256]{3,0,2,1:T(8,128)S(1)} %fusion.42, ...), kind=kOutput, calls=%fused_computation.1 | convolution fusion | flops 12190144 | bytes 9830400 | tf_op jit(solution)/shard_map/fn,n...->f.../dot_general | solution.py:50
  44.1 0.9 fusion.80
  45.0 0.9 fusion.78
  45.9 1.1 fusion.7
  46.9 1.0 fusion.6
  48.5 1.0 copy.47
  49.6 5.1 %all-to-all-start.2 = ((bf16[4,1,3,2,64,256]{5,4,2,3,1,0:T(8,128)(2,1)}), bf16[4,1,3,2,64,256]{5,4,2,3,1,0:T(8,128)(2,1)S(1)}, u32[]{:S(2)}, u32[]{:S(2)}) async-start(bf16[4,1,3,2,64,256]{5,4,2,3,1,0:T(8,128)(2,1)} %copy.47), calls=%async_computation.2 | async-start | bytes 1572864 | tf_op jit(solution)/shard_map/all_to_all | solution.py:85
  54.8 3.6 %collective-permute-start = (bf16[1,2,2,256,256]{4,3,2,1,0:T(8,128)(2,1)S(1)}, bf16[1,2,2,256,256]{4,3,2,1,0:T(8,128)(2,1)S(1)}, u32[]{:S(2)}, u32[]{:S(2)}) collective-permute-start(bf16[1,2,2,256,256]{4,3,2,1,0:T(8,128)(2,1)S(1)} %pad_maximum_fusion.1), channel_id=1, source_target_pairs={{0,1},{1,2},{2,3},{3,4},{4,5},{5,6},{6,7},{8,9},{9,10},{10,11},{11... | collective-permute-start | bytes 1572872 | tf_op jit(solution)/shard_map/ppermute | solution.py:15
  58.4 3.3 %collective-permute-start.1 = (bf16[1,2,2,256,256]{4,3,2,1,0:T(8,128)(2,1)S(1)}, bf16[1,2,2,256,256]{4,3,2,1,0:T(8,128)(2,1)S(1)}, u32[]{:S(2)}, u32[]{:S(2)}) collective-permute-start(bf16[1,2,2,256,256]{4,3,2,1,0:T(8,128)(2,1)S(1)} %pad_maximum_fusion.1), channel_id=1, source_target_pairs={{1,0},{2,1},{3,2},{4,3},{5,4},{6,5},{7,6},{9,8},{10,9},{11,10},{12... | collective-permute-start | bytes 1572872 | tf_op jit(solution)/shard_map/ppermute | solution.py:16
  61.7 3.0 %all-to-all-done.2 = bf16[4,1,3,2,64,256]{5,4,2,3,1,0:T(8,128)(2,1)S(1)} async-done(((bf16[4,1,3,2,64,256]{5,4,2,3,1,0:T(8,128)(2,1)}), bf16[4,1,3,2,64,256]{5,4,2,3,1,0:T(8,128)(2,1)S(1)}, u32[]{:S(2)}, u32[]{:S(2)}) %all-to-all-start.2) | async-done | bytes 786464 | tf_op jit(solution)/shard_map/all_to_all | solution.py:85
  66.8 15.9 %collective-permute-done.1 = bf16[1,2,2,256,256]{4,3,2,1,0:T(8,128)(2,1)S(1)} collective-permute-done((bf16[1,2,2,256,256]{4,3,2,1,0:T(8,128)(2,1)S(1)}, bf16[1,2,2,256,256]{4,3,2,1,0:T(8,128)(2,1)S(1)}, u32[]{:S(2)}, u32[]{:S(2)}) %collective-permute-start.1) | collective-permute-done | bytes 524320 | tf_op jit(solution)/shard_map/ppermute | solution.py:16
  87.1 1.9 %collective-permute-start.3 = (bf16[1,1,2,2,256,256]{5,4,3,2,1,0:T(8,128)(2,1)S(1)}, bf16[1,1,2,2,256,256]{5,4,3,2,1,0:T(8,128)(2,1)S(1)}, u32[]{:S(2)}, u32[]{:S(2)}) collective-permute-start(bf16[1,1,2,2,256,256]{5,4,3,2,1,0:T(8,128)(2,1)S(1)} %pad_maximum_fusion.3), channel_id=1, source_target_pairs={{1,0},{2,1},{3,2},{4,3},{5,4},{6,5},{7,6},{9,8},{10,9},{11,10},{12... | collective-permute-start | bytes 1572872 | tf_op jit(solution)/shard_map/ppermute | solution.py:24
  90.3 3.9 %collective-permute-start.2 = (bf16[1,1,2,2,256,256]{5,4,3,2,1,0:T(8,128)(2,1)S(1)}, bf16[1,1,2,2,256,256]{5,4,3,2,1,0:T(8,128)(2,1)S(1)}, u32[]{:S(2)}, u32[]{:S(2)}) collective-permute-start(bf16[1,1,2,2,256,256]{5,4,3,2,1,0:T(8,128)(2,1)S(1)} %pad_maximum_fusion.2), channel_id=1, source_target_pairs={{0,1},{1,2},{2,3},{3,4},{4,5},{5,6},{6,7},{8,9},{9,10},{10,11},{11... | collective-permute-start | bytes 1572872 | tf_op jit(solution)/shard_map/ppermute | solution.py:24
  95.2 18.9 %collective-permute-done.3 = bf16[1,1,2,2,256,256]{5,4,3,2,1,0:T(8,128)(2,1)S(1)} collective-permute-done((bf16[1,1,2,2,256,256]{5,4,3,2,1,0:T(8,128)(2,1)S(1)}, bf16[1,1,2,2,256,256]{5,4,3,2,1,0:T(8,128)(2,1)S(1)}, u32[]{:S(2)}, u32[]{:S(2)}) %collective-permute-start.3) | collective-permute-done | bytes 524320 | tf_op jit(solution)/shard_map/ppermute | solution.py:24
  116.7 0.8 fusion.39
  118.4 0.8 fusion.32
  (88 shorter events, 17.7 us)
Async XLA Ops:
  0.6 6.9 %copy-start.2 = (bf16[1,1,3,2,256,256]{5,4,3,2,1,0:T(8,128)(2,1)S(1)}, bf16[1,1,3,2,256,256]{5,4,3,2,1,0:T(8,128)(2,1)}, u32[]{:S(2)}) copy-start(bf16[1,1,3,2,256,256]{5,4,3,2,1,0:T(8,128)(2,1)} %param.4) | copy-start | bytes 2359300
  3.5 16.8 %all-to-all-start.1 = ((bf16[1,1,3,2,256,256]{5,2,3,1,0,4:T(4,128)(2,1)}), bf16[1,1,3,2,256,256]{5,2,3,1,0,4:T(4,128)(2,1)S(1)}, u32[]{:S(2)}, u32[]{:S(2)}) async-start(bf16[1,1,3,2,256,256]{5,2,3,1,0,4:T(4,128)(2,1)} %copy.44), calls=%async_computation.1 | async-start | bytes 2097152 | tf_op jit(solution)/shard_map/all_to_all | solution.py:105
  20.3 17.9 %all-to-all-start = ((bf16[1,1,3,2,256,256]{5,2,3,1,0,4:T(4,128)(2,1)}), bf16[1,1,3,2,256,256]{5,2,3,1,0,4:T(4,128)(2,1)S(1)}, u32[]{:S(2)}, u32[]{:S(2)}) async-start(bf16[1,1,3,2,256,256]{5,2,3,1,0,4:T(4,128)(2,1)} %copy.41), calls=%async_computation | async-start | bytes 2097152 | tf_op jit(solution)/shard_map/all_to_all | solution.py:104
  39.0 1.5 %copy-start.1 = (f32[8,3,64,256]{3,0,2,1:T(8,128)S(1)}, f32[8,3,64,256]{3,0,2,1:T(8,128)}, u32[]{:S(2)}) copy-start(f32[8,3,64,256]{3,0,2,1:T(8,128)} %fusion.43) | copy-start | bytes 4718596
  48.5 6.2 %copy-start.3 = (bf16[1,2,256,256]{3,2,1,0:T(8,128)(2,1)S(1)}, bf16[1,2,256,256]{3,2,1,0:T(8,128)(2,1)}, u32[]{:S(2)}) copy-start(bf16[1,2,256,256]{3,2,1,0:T(8,128)(2,1)} %param.7) | copy-start | bytes 786436
  48.5 6.2 %copy-start = (bf16[1,2,256,256]{3,2,1,0:T(8,128)(2,1)S(1)}, bf16[1,2,256,256]{3,2,1,0:T(8,128)(2,1)}, u32[]{:S(2)}) copy-start(bf16[1,2,256,256]{3,2,1,0:T(8,128)(2,1)} %param.6) | copy-start | bytes 786436
  49.6 15.1 %all-to-all-start.2 = ((bf16[4,1,3,2,64,256]{5,4,2,3,1,0:T(8,128)(2,1)}), bf16[4,1,3,2,64,256]{5,4,2,3,1,0:T(8,128)(2,1)S(1)}, u32[]{:S(2)}, u32[]{:S(2)}) async-start(bf16[4,1,3,2,64,256]{5,4,2,3,1,0:T(8,128)(2,1)} %copy.47), calls=%async_computation.2 | async-start | bytes 1572864 | tf_op jit(solution)/shard_map/all_to_all | solution.py:85
  54.8 29.6 %collective-permute-start = (bf16[1,2,2,256,256]{4,3,2,1,0:T(8,128)(2,1)S(1)}, bf16[1,2,2,256,256]{4,3,2,1,0:T(8,128)(2,1)S(1)}, u32[]{:S(2)}, u32[]{:S(2)}) collective-permute-start(bf16[1,2,2,256,256]{4,3,2,1,0:T(8,128)(2,1)S(1)} %pad_maximum_fusion.1), channel_id=1, source_target_pairs={{0,1},{1,2},{2,3},{3,4},{4,5},{5,6},{6,7},{8,9},{9,10},{10,11},{11... | collective-permute-start | bytes 1572872 | tf_op jit(solution)/shard_map/ppermute | solution.py:15
  58.4 24.4 %collective-permute-start.1 = (bf16[1,2,2,256,256]{4,3,2,1,0:T(8,128)(2,1)S(1)}, bf16[1,2,2,256,256]{4,3,2,1,0:T(8,128)(2,1)S(1)}, u32[]{:S(2)}, u32[]{:S(2)}) collective-permute-start(bf16[1,2,2,256,256]{4,3,2,1,0:T(8,128)(2,1)S(1)} %pad_maximum_fusion.1), channel_id=1, source_target_pairs={{1,0},{2,1},{3,2},{4,3},{5,4},{6,5},{7,6},{9,8},{10,9},{11,10},{12... | collective-permute-start | bytes 1572872 | tf_op jit(solution)/shard_map/ppermute | solution.py:16
  87.1 27.0 %collective-permute-start.3 = (bf16[1,1,2,2,256,256]{5,4,3,2,1,0:T(8,128)(2,1)S(1)}, bf16[1,1,2,2,256,256]{5,4,3,2,1,0:T(8,128)(2,1)S(1)}, u32[]{:S(2)}, u32[]{:S(2)}) collective-permute-start(bf16[1,1,2,2,256,256]{5,4,3,2,1,0:T(8,128)(2,1)S(1)} %pad_maximum_fusion.3), channel_id=1, source_target_pairs={{1,0},{2,1},{3,2},{4,3},{5,4},{6,5},{7,6},{9,8},{10,9},{11,10},{12... | collective-permute-start | bytes 1572872 | tf_op jit(solution)/shard_map/ppermute | solution.py:24
  90.3 25.3 %collective-permute-start.2 = (bf16[1,1,2,2,256,256]{5,4,3,2,1,0:T(8,128)(2,1)S(1)}, bf16[1,1,2,2,256,256]{5,4,3,2,1,0:T(8,128)(2,1)S(1)}, u32[]{:S(2)}, u32[]{:S(2)}) collective-permute-start(bf16[1,1,2,2,256,256]{5,4,3,2,1,0:T(8,128)(2,1)S(1)} %pad_maximum_fusion.2), channel_id=1, source_target_pairs={{0,1},{1,2},{2,3},{3,4},{4,5},{5,6},{6,7},{8,9},{9,10},{10,11},{11... | collective-permute-start | bytes 1572872 | tf_op jit(solution)/shard_map/ppermute | solution.py:24
where the time goes:
time: 120 us; the launch traced here: 119 us
  waiting for transfers between devices  58.3 us (49%)
  starting transfers between devices  27 us (22%)
  matrix products  22.5 us (19%)
  local copies, waits for them, and re-layouts  7.24 us (6%)
  other arithmetic  2.8 us (2%)
  between operations  1.33 us (1%)
    ppermute x2, waiting for transfers between devices, passed_along(): lax.ppermute(value, axis, [(source, source + steps) for source in range(i...  18.9 us
    ppermute x1, waiting for transfers between devices, extended(): after = lax.ppermute(initial, axis, down)  15.9 us
    dot_general x12, matrix products, transform(): jnp.einsum('fn,n...->f...', table, signal, precision=lax.Precision.HIGH)  11.5 us
    all_to_all x1, waiting for transfers between devices, per_device(): lax.all_to_all(g_greater, 'energy', split_axis=4, concat_axis=0, tiled=True)  11.1 us
    dot_general x56, matrix products, contract(): jnp.einsum(pattern, first_part, second_part, preferred_element_type=jnp.f...  11 us
    all_to_all x1, waiting for transfers between devices, per_device(): lax.all_to_all(g_lesser, 'energy', split_axis=4, concat_axis=0, tiled=True)  9.39 us
    ppermute x2, starting transfers between devices, passed_along(): lax.ppermute(value, axis, [(source, source + steps) for source in range(i...  5.87 us
    all_to_all x1, starting transfers between devices, per_device(): lax.all_to_all(g_lesser, 'energy', split_axis=4, concat_axis=0, tiled=True)  5.12 us
  transfers between devices with their start and end apart: 7, of which 5 were waited for; matrix products, arithmetic and copies ran while one was open for 10% of the time, Pallas kernels for 0%

commit v1 on v0

--- a/solution.py
+++ b/solution.py
@@ -3,6 +3,28 @@
 import jax.numpy as jnp
 from jax import lax
 from jax.sharding import PartitionSpec as P
+
+
+def cut_along(x, dim, peers):
+    before, after = (x.shape[:dim], x.shape[dim + 1 :])
+    return jnp.moveaxis(x.reshape(*before, peers, -1, *after), dim, 0)
+
+
+def laid_out(tiles, dim):
+    shape = list(tiles.shape[1:])
+    shape[dim] *= tiles.shape[0]
+    return jnp.moveaxis(tiles, 0, dim).reshape(shape)
+
+
+def sent_to_each(x, axis, split_dim, concat_dim):
+    peers, index = (lax.axis_size(axis), lax.axis_index(axis))
+    pieces = cut_along(x, split_dim, peers)
+    gathered = [pieces[index]]
+    for lap in range(1, peers):
+        sent = pieces[(index + lap) % peers]
+        gathered.append(lax.ppermute(sent, axis, [(i, (i + lap) % peers) for i in range(peers)]))
+    pieces = jnp.stack(gathered)[(index - jnp.arange(peers)) % peers]
+    return laid_out(pieces, concat_dim)
 
 
 def extended(shard, sides, width):
@@ -102,7 +124,7 @@
     middle = correlate(
         (
             lax.all_to_all(g_lesser, "energy", split_axis=4, concat_axis=0, tiled=True),
-            lax.all_to_all(g_greater, "energy", split_axis=4, concat_axis=0, tiled=True),
+            sent_to_each(g_greater, "energy", 4, 0),
         )
     )
     toward_above_y = complex_product(middle[:, :, 1], upper_middle) + complex_product(

time: 120 us -> 105 us (0.88)
  waiting for transfers between devices: 58.3 us -> 47.1 us
  starting transfers between devices: 27 us -> 23.6 us
    all_to_all x1 -> x0, waiting for transfers between devices: 11.1 us -> none  [per_device(): lax.all_to_all(g_greater, 'energy', split_axis=4, concat_axis=0, tiled=True)]
    all_to_all x1 -> x0, starting transfers between devices: 4.02 us -> none  [per_device(): lax.all_to_all(g_greater, 'energy', split_axis=4, concat_axis=0, tiled=True)]
    unnamed x10 -> x9, local copies, waits for them, and re-layouts: 4.55 us -> 2.29 us
    ppermute x0 -> x3, starting transfers between devices: none -> 2.05 us  [sent_to_each(): lax.ppermute(sent, axis, [(i, (i + lap) % peers) for i in range(peers)])]
    dynamic_slice x0 -> x1, local copies, waits for them, and re-layouts: none -> 1.34 us  [sent_to_each(): gathered = [pieces[index]]]
    gather x0 -> x2, local copies, waits for them, and re-layouts: none -> 1.21 us  [sent_to_each(): pieces = jnp.stack(gathered)[(index - jnp.arange(peers)) % peers]]
  transfers between devices with their start and end apart: 7 -> 9, of which waited for: 5 -> 5; matrix products, arithmetic and copies ran while one was open for 10% -> 13% of each run, Pallas kernels for 0% -> 0%
where the time goes in v1:
time: 105 us; the launch traced here: 104 us
  waiting for transfers between devices  47.1 us (45%)
  starting transfers between devices  23.6 us (22%)
  matrix products  22.5 us (21%)
  local copies, waits for them, and re-layouts  6.77 us (6%)
  other arithmetic  2.92 us (3%)
  between operations  1.42 us (1%)
    ppermute x2, waiting for transfers between devices, passed_along(): lax.ppermute(value, axis, [(source, source + steps) for source in range(i...  18.9 us
    ppermute x1, waiting for transfers between devices, extended(): after = lax.ppermute(initial, axis, down)  15.9 us
    dot_general x12, matrix products, transform(): jnp.einsum('fn,n...->f...', table, signal, precision=lax.Precision.HIGH)  11.5 us
    dot_general x56, matrix products, contract(): jnp.einsum(pattern, first_part, second_part, preferred_element_type=jnp.f...  11 us
    all_to_all x1, waiting for transfers between devices, per_device(): lax.all_to_all(g_lesser, 'energy', split_axis=4, concat_axis=0, tiled=True)  8.35 us
    ppermute x2, starting transfers between devices, passed_along(): lax.ppermute(value, axis, [(source, source + steps) for source in range(i...  5.87 us
    all_to_all x1, starting transfers between devices, per_device(): lax.all_to_all(g_lesser, 'energy', split_axis=4, concat_axis=0, tiled=True)  4.98 us
    all_to_all x1, starting transfers between devices, correlate(): lax.all_to_all(polar_entries, 'energy', split_axis=0, concat_axis=4, tile...  4 us
  transfers between devices with their start and end apart: 9, of which 5 were waited for; matrix products, arithmetic and copies ran while one was open for 13% of the time, Pallas kernels for 0%

profile of v1, /device:TPU:26, one launch (start us, length us, event | category | flops | bytes accessed | tf_op | source)
XLA Modules:
  0.0 104.4 jit_solution(4371863868725087674)
XLA Ops:
  0.7 1.3 %dynamic-slice_bitcast_fusion.3 = (bf16[1,1,1,3,2,64,256]{6,5,4,3,0,2,1:T(8,128)(2,1)S(1)}, bf16[1,1,3,2,64,256]{5,4,3,2,1,0:T(8,128)(2,1)S(1)}, bf16[1,1,3,2,64...) fusion(bf16[1,1,3,2,4,64,256]{6,5,4,3,2,1,0:T(8,128)(2,1)} %bitcast.406, s32[]{:T(128)S(6)} %select_n.84, ...), kind=kLoop, calls=%fused_computation.121 | loop fusion | bytes 1572880 | tf_op jit(solution)/shard_map/dynamic_slice | solution.py:22
  2.7 1.4 %collective-permute-start.3 = (bf16[1,1,3,2,64,256]{5,4,3,2,1,0:T(8,128)(2,1)S(1)}, bf16[1,1,3,2,64,256]{5,4,3,2,1,0:T(8,128)(2,1)S(1)}, u32[]{:S(2)}, u32[]{:S(2)}) collective-permute-start(bf16[1,1,3,2,64,256]{5,4,3,2,1,0:T(8,128)(2,1)S(1)} %get-tuple-element.10), channel_id=1, source_target_pairs={{0,24},{8,0},{16,8},{24,16},{1,25},{9,1},{17,9},{25,17},{2,26},{10... | collective-permute-start | bytes 589832 | tf_op jit(solution)/shard_map/ppermute | solution.py:25
  4.1 1.7 %copy.47 = bf16[1,1,3,2,256,256]{5,2,3,1,0,4:T(4,128)(2,1)} copy(bf16[1,1,3,2,256,256]{5,4,3,2,1,0:T(8,128)(2,1)S(1)} %copy-done.2) | data formatting | bytes 1572864 | tf_op args[0]
  5.7 5.0 %all-to-all-start = ((bf16[1,1,3,2,256,256]{5,2,3,1,0,4:T(4,128)(2,1)}), bf16[1,1,3,2,256,256]{5,2,3,1,0,4:T(4,128)(2,1)S(1)}, u32[]{:S(2)}, u32[]{:S(2)}) async-start(bf16[1,1,3,2,256,256]{5,2,3,1,0,4:T(4,128)(2,1)} %copy.47), calls=%async_computation | async-start | bytes 2097152 | tf_op jit(solution)/shard_map/all_to_all | solution.py:126
  10.8 0.9 collective-permute-done.3
  13.7 1.9 %fusion.44 = f32[8,3,64,256]{3,0,2,1:T(8,128)} fusion(bf16[4,1,3,2,64,256]{5,0,4,2,3,1:T(4,128)(2,1)S(1)} %bitcast.377), kind=kOutput, calls=%fused_computation.105 | convolution fusion | flops 9437632 | bytes 1966080 | tf_op jit(solution)/shard_map/fn,n...->f.../dot_general | solution.py:72
  16.4 8.3 %all-to-all-done = bf16[1,1,3,2,256,256]{5,2,3,1,0,4:T(4,128)(2,1)S(1)} async-done(((bf16[1,1,3,2,256,256]{5,2,3,1,0,4:T(4,128)(2,1)}), bf16[1,1,3,2,256,256]{5,2,3,1,0,4:T(4,128)(2,1)S(1)}, u32[]{:S(2)}, u32[]{:S(2)}) %all-to-all-start) | async-done | bytes 786464 | tf_op jit(solution)/shard_map/all_to_all | solution.py:126
  27.0 0.8 convolution_subtract_fusion.1
  29.2 1.2 %multiply_subtract_fusion = (f32[8,3,64,256]{3,0,2,1:T(8,128)S(1)}, f32[8,3,64,256]{3,0,2,1:T(8,128)S(1)}) fusion(f32[8,3,64,256]{3,0,2,1:T(8,128)S(1)} %convolution_add_fusion, f32[8,3,64,256]{3,0,2,1:T(8,128)S(1)} %convolution_subtract_fusion.1, f32[8,3,64,256]{3,0,2,1:T(8,128)S(1)} %convolution_add_fusion.1, f32[8,3,64,256]{3,0,2,1:T(8,128)S(1)} %copy-done.1, ...), kind=kOutput, calls=%fused_computation.2 | convolution fusion | flops 12190144 | bytes 9830400 | tf_op jit(solution)/shard_map/fn,n...->f.../dot_general | solution.py:72
  30.5 0.9 fusion.80
  31.3 0.9 fusion.78
  32.2 1.1 %fusion.7 = bf16[4,1,3,1,64,256]{5,0,4,2,3,1:T(4,128)(2,1)S(1)} fusion(f32[4,3,64,256]{3,0,2,1:T(4,128)S(1)} %fusion.80, f32[8,3,64,256]{3,0,2,1:T(8,128)S(1)} %get-tuple-element.3, s32[4]{0:T(128)S(1)} %iota_add_fusion), kind=kOutput, calls=%fused_computation.16 | convolution fusion | flops 10420672 | bytes 2752528 | tf_op jit(solution)/shard_map/fn,n...->f.../dot_general | solution.py:72
  33.3 1.0 fusion.6
  34.9 1.0 copy.55
  35.9 4.0 %all-to-all-start.1 = ((bf16[4,1,3,2,64,256]{5,4,2,3,1,0:T(8,128)(2,1)}), bf16[4,1,3,2,64,256]{5,4,2,3,1,0:T(8,128)(2,1)S(1)}, u32[]{:S(2)}, u32[]{:S(2)}) async-start(bf16[4,1,3,2,64,256]{5,4,2,3,1,0:T(8,128)(2,1)} %copy.55), calls=%async_computation.1 | async-start | bytes 1572864 | tf_op jit(solution)/shard_map/all_to_all | solution.py:107
  40.0 3.4 %collective-permute-start = (bf16[1,2,2,256,256]{4,3,2,1,0:T(8,128)(2,1)S(1)}, bf16[1,2,2,256,256]{4,3,2,1,0:T(8,128)(2,1)S(1)}, u32[]{:S(2)}, u32[]{:S(2)}) collective-permute-start(bf16[1,2,2,256,256]{4,3,2,1,0:T(8,128)(2,1)S(1)} %pad_maximum_fusion.1), channel_id=1, source_target_pairs={{0,1},{1,2},{2,3},{3,4},{4,5},{5,6},{6,7},{8,9},{9,10},{10,11},{11... | collective-permute-start | bytes 1572872 | tf_op jit(solution)/shard_map/ppermute | solution.py:37
  43.4 3.3 %collective-permute-start.4 = (bf16[1,2,2,256,256]{4,3,2,1,0:T(8,128)(2,1)S(1)}, bf16[1,2,2,256,256]{4,3,2,1,0:T(8,128)(2,1)S(1)}, u32[]{:S(2)}, u32[]{:S(2)}) collective-permute-start(bf16[1,2,2,256,256]{4,3,2,1,0:T(8,128)(2,1)S(1)} %pad_maximum_fusion.1), channel_id=1, source_target_pairs={{1,0},{2,1},{3,2},{4,3},{5,4},{6,5},{7,6},{9,8},{10,9},{11,10},{12... | collective-permute-start | bytes 1572872 | tf_op jit(solution)/shard_map/ppermute | solution.py:38
  46.8 3.1 %all-to-all-done.1 = bf16[4,1,3,2,64,256]{5,4,2,3,1,0:T(8,128)(2,1)S(1)} async-done(((bf16[4,1,3,2,64,256]{5,4,2,3,1,0:T(8,128)(2,1)}), bf16[4,1,3,2,64,256]{5,4,2,3,1,0:T(8,128)(2,1)S(1)}, u32[]{:S(2)}, u32[]{:S(2)}) %all-to-all-start.1) | async-done | bytes 786464 | tf_op jit(solution)/shard_map/all_to_all | solution.py:107
  52.1 15.9 %collective-permute-done.4 = bf16[1,2,2,256,256]{4,3,2,1,0:T(8,128)(2,1)S(1)} collective-permute-done((bf16[1,2,2,256,256]{4,3,2,1,0:T(8,128)(2,1)S(1)}, bf16[1,2,2,256,256]{4,3,2,1,0:T(8,128)(2,1)S(1)}, u32[]{:S(2)}, u32[]{:S(2)}) %collective-permute-start.4) | collective-permute-done | bytes 524320 | tf_op jit(solution)/shard_map/ppermute | solution.py:38
  72.3 1.9 %collective-permute-start.6 = (bf16[1,1,2,2,256,256]{5,4,3,2,1,0:T(8,128)(2,1)S(1)}, bf16[1,1,2,2,256,256]{5,4,3,2,1,0:T(8,128)(2,1)S(1)}, u32[]{:S(2)}, u32[]{:S(2)}) collective-permute-start(bf16[1,1,2,2,256,256]{5,4,3,2,1,0:T(8,128)(2,1)S(1)} %pad_maximum_fusion.3), channel_id=1, source_target_pairs={{1,0},{2,1},{3,2},{4,3},{5,4},{6,5},{7,6},{9,8},{10,9},{11,10},{12... | collective-permute-start | bytes 1572872 | tf_op jit(solution)/shard_map/ppermute | solution.py:46
  75.6 3.9 %collective-permute-start.5 = (bf16[1,1,2,2,256,256]{5,4,3,2,1,0:T(8,128)(2,1)S(1)}, bf16[1,1,2,2,256,256]{5,4,3,2,1,0:T(8,128)(2,1)S(1)}, u32[]{:S(2)}, u32[]{:S(2)}) collective-permute-start(bf16[1,1,2,2,256,256]{5,4,3,2,1,0:T(8,128)(2,1)S(1)} %pad_maximum_fusion.2), channel_id=1, source_target_pairs={{0,1},{1,2},{2,3},{3,4},{4,5},{5,6},{6,7},{8,9},{9,10},{10,11},{11... | collective-permute-start | bytes 1572872 | tf_op jit(solution)/shard_map/ppermute | solution.py:46
  80.5 18.9 %collective-permute-done.6 = bf16[1,1,2,2,256,256]{5,4,3,2,1,0:T(8,128)(2,1)S(1)} collective-permute-done((bf16[1,1,2,2,256,256]{5,4,3,2,1,0:T(8,128)(2,1)S(1)}, bf16[1,1,2,2,256,256]{5,4,3,2,1,0:T(8,128)(2,1)S(1)}, u32[]{:S(2)}, u32[]{:S(2)}) %collective-permute-start.6) | collective-permute-done | bytes 524320 | tf_op jit(solution)/shard_map/ppermute | solution.py:46
  101.9 0.8 fusion.39
  103.6 0.8 fusion.32
  (96 shorter events, 19.5 us)
Async XLA Ops:
  0.6 3.5 %copy-start.2 = (bf16[1,1,3,2,256,256]{5,4,3,2,1,0:T(8,128)(2,1)S(1)}, bf16[1,1,3,2,256,256]{5,4,3,2,1,0:T(8,128)(2,1)}, u32[]{:S(2)}) copy-start(bf16[1,1,3,2,256,256]{5,4,3,2,1,0:T(8,128)(2,1)} %param.4) | copy-start | bytes 2359300
  2.0 8.7 %collective-permute-start.1 = (bf16[1,1,3,2,64,256]{5,4,3,2,1,0:T(8,128)(2,1)S(1)}, bf16[1,1,3,2,64,256]{5,4,3,2,1,0:T(8,128)(2,1)S(1)}, u32[]{:S(2)}, u32[]{:S(2)}) collective-permute-start(bf16[1,1,3,2,64,256]{5,4,3,2,1,0:T(8,128)(2,1)S(1)} %get-tuple-element.9), channel_id=1, source_target_pairs={{0,8},{8,16},{16,24},{24,0},{1,9},{9,17},{17,25},{25,1},{2,10},{10... | collective-permute-start | bytes 589832 | tf_op jit(solution)/shard_map/ppermute | solution.py:25
  2.1 8.7 %collective-permute-start.2 = (bf16[1,1,3,2,64,256]{5,4,3,2,1,0:T(8,128)(2,1)S(1)}, bf16[1,1,3,2,64,256]{5,4,3,2,1,0:T(8,128)(2,1)S(1)}, u32[]{:S(2)}, u32[]{:S(2)}) collective-permute-start(bf16[1,1,3,2,64,256]{5,4,3,2,1,0:T(8,128)(2,1)S(1)} %get-tuple-element.8), channel_id=1, source_target_pairs={{0,16},{8,24},{16,0},{24,8},{1,17},{9,25},{17,1},{25,9},{2,18},{10... | collective-permute-start | bytes 589832 | tf_op jit(solution)/shard_map/ppermute | solution.py:25
  2.7 9.0 %collective-permute-start.3 = (bf16[1,1,3,2,64,256]{5,4,3,2,1,0:T(8,128)(2,1)S(1)}, bf16[1,1,3,2,64,256]{5,4,3,2,1,0:T(8,128)(2,1)S(1)}, u32[]{:S(2)}, u32[]{:S(2)}) collective-permute-start(bf16[1,1,3,2,64,256]{5,4,3,2,1,0:T(8,128)(2,1)S(1)} %get-tuple-element.10), channel_id=1, source_target_pairs={{0,24},{8,0},{16,8},{24,16},{1,25},{9,1},{17,9},{25,17},{2,26},{10... | collective-permute-start | bytes 589832 | tf_op jit(solution)/shard_map/ppermute | solution.py:25
  5.7 19.0 %all-to-all-start = ((bf16[1,1,3,2,256,256]{5,2,3,1,0,4:T(4,128)(2,1)}), bf16[1,1,3,2,256,256]{5,2,3,1,0,4:T(4,128)(2,1)S(1)}, u32[]{:S(2)}, u32[]{:S(2)}) async-start(bf16[1,1,3,2,256,256]{5,2,3,1,0,4:T(4,128)(2,1)} %copy.47), calls=%async_computation | async-start | bytes 2097152 | tf_op jit(solution)/shard_map/all_to_all | solution.py:126
  27.8 1.4 %copy-start.1 = (f32[8,3,64,256]{3,0,2,1:T(8,128)S(1)}, f32[8,3,64,256]{3,0,2,1:T(8,128)}, u32[]{:S(2)}) copy-start(f32[8,3,64,256]{3,0,2,1:T(8,128)} %fusion.44) | copy-start | bytes 4718596
  34.9 5.0 %copy-start.3 = (bf16[1,2,256,256]{3,2,1,0:T(8,128)(2,1)S(1)}, bf16[1,2,256,256]{3,2,1,0:T(8,128)(2,1)}, u32[]{:S(2)}) copy-start(bf16[1,2,256,256]{3,2,1,0:T(8,128)(2,1)} %param.7) | copy-start | bytes 786436
  34.9 5.1 %copy-start = (bf16[1,2,256,256]{3,2,1,0:T(8,128)(2,1)S(1)}, bf16[1,2,256,256]{3,2,1,0:T(8,128)(2,1)}, u32[]{:S(2)}) copy-start(bf16[1,2,256,256]{3,2,1,0:T(8,128)(2,1)} %param.6) | copy-start | bytes 786436
  35.9 14.0 %all-to-all-start.1 = ((bf16[4,1,3,2,64,256]{5,4,2,3,1,0:T(8,128)(2,1)}), bf16[4,1,3,2,64,256]{5,4,2,3,1,0:T(8,128)(2,1)S(1)}, u32[]{:S(2)}, u32[]{:S(2)}) async-start(bf16[4,1,3,2,64,256]{5,4,2,3,1,0:T(8,128)(2,1)} %copy.55), calls=%async_computation.1 | async-start | bytes 1572864 | tf_op jit(solution)/shard_map/all_to_all | solution.py:107
  40.0 29.6 %collective-permute-start = (bf16[1,2,2,256,256]{4,3,2,1,0:T(8,128)(2,1)S(1)}, bf16[1,2,2,256,256]{4,3,2,1,0:T(8,128)(2,1)S(1)}, u32[]{:S(2)}, u32[]{:S(2)}) collective-permute-start(bf16[1,2,2,256,256]{4,3,2,1,0:T(8,128)(2,1)S(1)} %pad_maximum_fusion.1), channel_id=1, source_target_pairs={{0,1},{1,2},{2,3},{3,4},{4,5},{5,6},{6,7},{8,9},{9,10},{10,11},{11... | collective-permute-start | bytes 1572872 | tf_op jit(solution)/shard_map/ppermute | solution.py:37
  43.4 24.5 %collective-permute-start.4 = (bf16[1,2,2,256,256]{4,3,2,1,0:T(8,128)(2,1)S(1)}, bf16[1,2,2,256,256]{4,3,2,1,0:T(8,128)(2,1)S(1)}, u32[]{:S(2)}, u32[]{:S(2)}) collective-permute-start(bf16[1,2,2,256,256]{4,3,2,1,0:T(8,128)(2,1)S(1)} %pad_maximum_fusion.1), channel_id=1, source_target_pairs={{1,0},{2,1},{3,2},{4,3},{5,4},{6,5},{7,6},{9,8},{10,9},{11,10},{12... | collective-permute-start | bytes 1572872 | tf_op jit(solution)/shard_map/ppermute | solution.py:38
  72.3 27.0 %collective-permute-start.6 = (bf16[1,1,2,2,256,256]{5,4,3,2,1,0:T(8,128)(2,1)S(1)}, bf16[1,1,2,2,256,256]{5,4,3,2,1,0:T(8,128)(2,1)S(1)}, u32[]{:S(2)}, u32[]{:S(2)}) collective-permute-start(bf16[1,1,2,2,256,256]{5,4,3,2,1,0:T(8,128)(2,1)S(1)} %pad_maximum_fusion.3), channel_id=1, source_target_pairs={{1,0},{2,1},{3,2},{4,3},{5,4},{6,5},{7,6},{9,8},{10,9},{11,10},{12... | collective-permute-start | bytes 1572872 | tf_op jit(solution)/shard_map/ppermute | solution.py:46
  75.6 25.3 %collective-permute-start.5 = (bf16[1,1,2,2,256,256]{5,4,3,2,1,0:T(8,128)(2,1)S(1)}, bf16[1,1,2,2,256,256]{5,4,3,2,1,0:T(8,128)(2,1)S(1)}, u32[]{:S(2)}, u32[]{:S(2)}) collective-permute-start(bf16[1,1,2,2,256,256]{5,4,3,2,1,0:T(8,128)(2,1)S(1)} %pad_maximum_fusion.2), channel_id=1, source_target_pairs={{0,1},{1,2},{2,3},{3,4},{4,5},{5,6},{6,7},{8,9},{9,10},{10,11},{11... | collective-permute-start | bytes 1572872 | tf_op jit(solution)/shard_map/ppermute | solution.py:46
